TPU v7x, 256 devices: a whole 4x4x8 slice. The times are simulated.
256 devices in a mesh: fn: 8 (over z_hi, core), pt: 32 (over x, y, z_lo).
Axes of the slice: x: 4, y: 4, z: 8 (z_hi: 4, z_lo: 2; z = z_hi * 2 + z_lo), core: 2. Of those that a mesh axis runs over, the one named last changes fastest.
Arguments:
- functions: bfloat16 [16384, 4096], P(('fn', 'pt')), may hold values from -6 to 6
- branch_in: bfloat16 [4096, 256], replicated, may hold values from -0.09375 to 0.09375
- branch_out: bfloat16 [256, 128], replicated, may hold values from -0.375 to 0.375
- branch_tangent: bfloat16 [256, 128], replicated, may hold values from -0.375 to 0.375
- points: float32 [2, 32768], P(None, ('pt', 'fn')), may hold values from 0 to 1
- trunk_in: float32 [2, 256], replicated, may hold values from -4 to 4
- trunk_bias: float32 [256], replicated, may hold values from -1 to 1
- trunk_out: bfloat16 [256, 128], replicated, may hold values from -0.375 to 0.375
- trunk_tangent: bfloat16 [256, 128], replicated, may hold values from -0.375 to 0.375
- slopes: bfloat16 [2, 16384, 32768], P(None, 'fn', 'pt'), may hold values from -4 to 4
Outputs:
- row_grad: float32 [16384, 128], P(('fn', 'pt'))
- branch_grad: float32 [256, 128], replicated
- trunk_grad: float32 [256, 128], replicated
All inputs are finite; a program needn't handle non-finite values.
Results may differ from a plain program's by a relative error of at most 0.0041.
Values may be sent and summed in bfloat16 or wider, within the bound.
No kernel may reach another device: no remote copies, remote signals or barrier semaphores. Data moves between devices by JAX's collectives and lax.ppermute only.
A program may use at most 192 MiB of HBM per device.

v0:
```python
import jax
import jax.numpy as jnp
from jax import lax
from jax.sharding import PartitionSpec as P


def jet_features(points, trunk_in, trunk_bias):
    preact = (
        points[0][:, None] * trunk_in[0][None, :]
        + points[1][:, None] * trunk_in[1][None, :]
        + trunk_bias[None, :]
    )
    tanh_value = jnp.tanh(preact)
    first_deriv = 1.0 - tanh_value * tanh_value
    second_deriv = -2.0 * tanh_value * first_deriv
    square_sum = trunk_in[0] * trunk_in[0] + trunk_in[1] * trunk_in[1]
    return jnp.stack(
        [
            second_deriv * square_sum[None, :],
            first_deriv * trunk_in[0][None, :],
            first_deriv * trunk_in[1][None, :],
        ]
    ).astype(jnp.bfloat16)


def project(source, matrix):
    return jnp.einsum("cjk,kp->cjp", source, matrix, preferred_element_type=jnp.float32).astype(
        jnp.bfloat16
    )


def local(
    functions,
    branch_in,
    branch_out,
    branch_tangent,
    points,
    trunk_in,
    trunk_bias,
    trunk_out,
    trunk_tangent,
    slopes,
):
    highest = lax.Precision.HIGHEST
    total_rows = functions.shape[0] * lax.axis_size("fn") * lax.axis_size("pt")
    total_points = points.shape[1] * lax.axis_size("fn") * lax.axis_size("pt")
    hidden = jnp.tanh(jnp.dot(functions, branch_in, preferred_element_type=jnp.float32)).astype(
        jnp.bfloat16
    )
    latent = jnp.dot(hidden, branch_out, preferred_element_type=jnp.float32).astype(jnp.bfloat16)
    latent_tan = jnp.dot(hidden, branch_tangent, preferred_element_type=jnp.float32).astype(
        jnp.bfloat16
    )
    stacked = lax.all_gather(jnp.stack([latent, latent_tan]), "pt", axis=1, tiled=True)
    features = jet_features(points, trunk_in, trunk_bias)
    local_pair = jnp.stack([project(features, trunk_out), project(features, trunk_tangent)])
    gathered = lax.all_gather(local_pair, "fn", axis=2, tiled=True)
    trunk_val = gathered[0]
    trunk_tan = gathered[1]
    row_latent = stacked[0]
    row_factors = jnp.concatenate([stacked[0], stacked[1]], axis=1)
    point_factors = jnp.concatenate([trunk_tan, trunk_val], axis=2)
    response = jnp.einsum(
        "ik,cjk->cij", row_factors, point_factors, preferred_element_type=jnp.float32
    )
    slope_pair = slopes.astype(jnp.float32)
    tangent = response[0] + slope_pair[0] * response[1] + slope_pair[1] * response[2]
    scaled = tangent * (1.0 / total_points)
    weights = jnp.stack([scaled, slope_pair[0] * scaled, slope_pair[1] * scaled]).astype(
        jnp.bfloat16
    )
    weight_block = weights
    row_grad = lax.psum_scatter(
        jnp.einsum("cij,cjp->ip", weight_block, trunk_val, preferred_element_type=jnp.float32),
        "pt",
        scatter_dimension=0,
        tiled=True,
    )
    weight_block = weights
    summed = jnp.einsum("cij,ip->jcp", weight_block, row_latent, preferred_element_type=jnp.float32)
    point_grad = lax.psum_scatter(
        summed * (1.0 / total_rows), "fn", scatter_dimension=0, tiled=True
    )
    trunk_grad = jnp.einsum(
        "cjk,jcp->kp", features.astype(jnp.float32), point_grad, precision=highest
    )
    branch_grad = jnp.dot(hidden.astype(jnp.float32).T, row_grad, precision=highest) * (
        1.0 / total_rows
    )
    branch_grad, trunk_grad = lax.psum((branch_grad, trunk_grad), ("fn", "pt"))
    return (row_grad, branch_grad, trunk_grad)


def solution(mesh):
    in_specs = (
        P(("fn", "pt"), None),
        P(),
        P(),
        P(),
        P(None, ("pt", "fn")),
        P(),
        P(),
        P(),
        P(),
        P(None, "fn", "pt"),
    )
    out_specs = (P(("fn", "pt"), None), P(), P())
    return jax.shard_map(local, mesh=mesh, in_specs=in_specs, out_specs=out_specs, check_vma=False)
```

profile of v0, /device:TPU:8, one launch (start us, length us, event | category | flops | bytes accessed | tf_op | source)
XLA Modules:
  0.0 728.2 jit_solution(10988406394103816467)
XLA Ops:
  7.2 0.0 copy-start
  7.2 0.0 all-gather.5.cloned.1.call-start
  7.2 1.5 copy-done
  8.8 1.5 fusion.11
  10.3 1.0 fusion.13
  11.2 1.0 fusion.12
  12.2 0.6 pad_maximum_fusion.9
  12.9 0.0 all-gather.5.cloned.1.call-update
  12.9 0.0 all-gather.3.cloned.1.call-start
  12.9 0.8 slice_bitcast_fusion.5
  13.7 0.8 multiply_add_fusion
  14.5 0.8 multiply_convert_fusion.4
  15.3 1.0 fusion.10
  16.3 1.0 fusion.9
  17.4 0.7 pad_maximum_fusion.8
  18.1 0.0 all-gather.3.cloned.1.call-update
  18.1 0.0 reduce-scatter.3.cloned.1.call-start
  18.1 11.7 %copy.13 = bf16[2,2048,1024]{1,2,0:T(8,128)(2,1)} copy(bf16[2,2048,1024]{2,1,0:T(8,128)(2,1)} %param.19) | data formatting | bytes 16777216 | tf_op args[9]
  29.9 11.3 %convert_element_type.27 = f32[2,2048,1024]{1,2,0:T(8,128)} convert(bf16[2,2048,1024]{1,2,0:T(8,128)(2,1)} %copy.13) | non-fusion elementwise | flops 4194304 | bytes 25165824 | tf_op jit(solution)/shard_map/convert_element_type | solution.py:66
  41.1 124.2 %all-gather.5.cloned.1.call-done = bf16[2,2048,128]{2,1,0:T(8,128)(2,1)} async-done(((bf16[2,64,128]{2,1,0:T(8,128)(2,1)}), bf16[2,2048,128]{2,1,0:T(8,128)(2,1)}) %all-gather.5.cloned.1.call-update) | async-done | bytes 1048592 | tf_op jit(solution)/shard_map/all_gather | solution.py:54
  165.4 1.3 slice_bitcast_fusion.3
  166.6 38.8 %all-gather.3.cloned.1.call-done = bf16[2,3,1024,128]{3,2,1,0:T(8,128)(2,1)} async-done(((bf16[2,3,128,128]{3,2,1,0:T(8,128)(2,1)}), bf16[2,3,1024,128]{3,2,1,0:T(8,128)(2,1)}) %all-gather.3.cloned.1.call-update) | async-done | bytes 1572880 | tf_op jit(solution)/shard_map/all_gather | solution.py:57
  205.4 1.5 slice_bitcast_fusion.1
  206.9 10.2 %convolution_bitcast_fusion = f32[3,2048,1024]{1,2,0:T(8,128)} fusion(bf16[3,1024,128]{2,1,0:T(8,128)(2,1)S(1)} %get-tuple-element.10, bf16[3,1024,128]{2,1,0:T(8,128)(2,1)S(1)} %get-tuple-element.9, bf16[2048,128]{1,0:T(8,128)(2,1)S(1)} %get-tuple-element.12, bf16[2048,128]{1,0:T(8,128)(2,1)S(1)} %get-tuple-element.11), kind=kOutput, calls=%fused_computation.1 | convolution fusion | flops 3226468352 | bytes 27787264 | tf_op jit(solution)/shard_map/ik,cjk->cij/dot_general | solution.py:63
  217.1 20.8 %fusion.23 = (bf16[1,2048,1024]{1,2,0:T(8,128)(2,1)}, f32[1,2048,1024]{1,2,0:T(8,128)}) fusion(f32[3,2048,1024]{1,2,0:T(8,128)} %convolution_bitcast_fusion, f32[2,2048,1024]{1,2,0:T(8,128)} %convert_element_type.27), kind=kLoop, calls=%fused_computation.53 | loop fusion | flops 12582912 | bytes 54525952 | tf_op jit(solution)/shard_map/convert
  238.0 0.0 copy-start.2
  238.0 0.0 copy-start.5
  238.0 10.3 %multiply_convert_fusion.1 = (bf16[1,2048,1024]{1,2,0:T(8,128)(2,1)S(1)}, bf16[1,2048,1024]{1,2,0:T(8,128)(2,1)S(1)}) fusion(f32[1,2048,1024]{1,2,0:T(8,128)} %get-tuple-element.6, f32[2,2048,1024]{1,2,0:T(8,128)} %convert_element_type.27), kind=kLoop, calls=%fused_computation.8 | loop fusion | flops 8388608 | bytes 33554432 | tf_op jit(solution)/shard_map/convert.1
  248.3 0.0 copy-start.3
  248.3 0.0 copy-start.4
  248.3 2.0 copy-done.3
  250.3 1.3 copy-done.4
  251.5 0.0 copy-done.2
  251.5 0.0 copy-done.5
  251.5 0.0 copy-start.6
  251.5 4.9 fusion.5
  256.4 0.0 reduce-scatter.3.cloned.1.call-update
  256.4 0.0 reduce-scatter.5.cloned.1.call-start
  256.5 0.0 copy-done.6
  256.5 0.0 copy-start.1
  256.5 7.5 %multiply_bitcast_fusion = f32[1024,3,128]{2,0,1:T(8,128)} fusion(bf16[1,2048,1024]{1,2,0:T(8,128)(2,1)} %copy-done.4, bf16[1,2048,1024]{1,2,0:T(8,128)(2,1)} %copy-done.3, bf16[1,2048,1024]{1,2,0:T(8,128)(2,1)} %get-tuple-element.5, bf16[2,2048,128]{2,1,0:T(8,128)(2,1)S(1)} %copy-done.6), kind=kOutput, calls=%fused_computation.15 | convolution fusion | flops 1648754688 | bytes 14680064 | tf_op jit(solution)/shard_map/cij,ip->jcp/dot_general | solution.py:80
  264.0 0.0 reduce-scatter.5.cloned.1.call-update
  264.0 0.0 all-reduce.3.cloned.1.call-start
  264.1 151.3 %reduce-scatter.3.cloned.1.call-done = f32[64,128]{1,0:T(8,128)} async-done(((f32[2048,128]{1,0:T(8,128)}), f32[64,128]{1,0:T(8,128)}) %reduce-scatter.3.cloned.1.call-update) | async-done | bytes 32784 | tf_op jit(solution)/shard_map/reduce_scatter | solution.py:73
  415.4 1.7 convolution_multiply_fusion
  417.1 41.8 %reduce-scatter.5.cloned.1.call-done = f32[128,3,128]{2,0,1:T(8,128)} async-done(((f32[1024,3,128]{2,0,1:T(8,128)}), f32[128,3,128]{2,0,1:T(8,128)}) %reduce-scatter.5.cloned.1.call-update) | async-done | bytes 196624 | tf_op jit(solution)/shard_map/reduce_scatter | solution.py:81
  458.9 2.0 convolution_bitcast_fusion.1
  460.9 0.0 all-reduce.3.cloned.1.call-update
  460.9 257.6 %all-reduce.3.cloned.1.call-done = (f32[256,128]{1,0:T(8,128)}, f32[256,128]{1,0:T(8,128)}) async-done(((f32[256,128]{1,0:T(8,128)}, f32[256,128]{1,0:T(8,128)}), (f32[256,128]{1,0:T(8,128)}, f32[256,128]{1,0:T(8,128)})) %all-reduce.3.cloned.1.call-update) | async-done | bytes 262160 | tf_op jit(solution)/shard_map/psum | solution.py:90
  718.5 1.6 copy.20
  720.1 1.6 copy.21
  721.7 0.0 copy-done.1
Async XLA Ops:
  7.2 1.6 copy-start
  7.2 158.2 %all-gather.5.cloned.1.call-start = ((), (), s32[]{:S(2)}) async-start(), calls=%async_computation.3 | async-start | bytes 1081344 | tf_op jit(solution)/shard_map/all_gather | solution.py:54
  12.9 192.5 %all-gather.3.cloned.1.call-start = ((), (), s32[]{:S(2)}) async-start(), calls=%async_computation.2 | async-start | bytes 1769472 | tf_op jit(solution)/shard_map/all_gather | solution.py:57
  18.1 397.3 %reduce-scatter.3.cloned.1.call-start = ((), (), s32[]{:S(2)}) async-start(), calls=%async_computation.4 | async-start | bytes 1081344 | tf_op jit(solution)/shard_map/reduce_scatter | solution.py:73
  238.0 13.6 %copy-start.2 = (bf16[1,2048,1024]{1,2,0:T(8,128)(2,1)S(1)}, bf16[1,2048,1024]{1,2,0:T(8,128)(2,1)}, u32[]{:S(2)}) copy-start(bf16[1,2048,1024]{1,2,0:T(8,128)(2,1)} %get-tuple-element.5) | copy-start | bytes 12582916
  238.0 13.6 %copy-start.5 = (bf16[2,3,1024,128]{3,2,1,0:T(8,128)(2,1)S(1)}, bf16[2,3,1024,128]{3,2,1,0:T(8,128)(2,1)}, u32[]{:S(2)}) copy-start(bf16[2,3,1024,128]{3,2,1,0:T(8,128)(2,1)} %all-gather.3.cloned.1.call-done) | copy-start | bytes 4718596
  248.3 2.0 copy-start.3
  248.3 3.3 copy-start.4
  251.5 5.0 copy-start.6
  256.4 202.5 %reduce-scatter.5.cloned.1.call-start = ((), (), s32[]{:S(2)}) async-start(), calls=%async_computation.5 | async-start | bytes 1769472 | tf_op jit(solution)/shard_map/reduce_scatter | solution.py:81
  256.5 465.2 %copy-start.1 = (bf16[4096,256]{1,0:T(8,128)(2,1)S(1)}, bf16[4096,256]{1,0:T(8,128)(2,1)}, u32[]{:S(2)}) copy-start(bf16[4096,256]{1,0:T(8,128)(2,1)} %param.11) | copy-start | bytes 6291460
  264.0 454.5 %all-reduce.3.cloned.1.call-start = ((), (), s32[]{:S(2)}) async-start(), calls=%async_computation.6 | async-start | bytes 524288 | tf_op jit(solution)/shard_map/psum | solution.py:90
Sparse Core Ops, SparseCore 0:
  13.0 152.3 all-gather.4
  167.2 38.1 all-gather.2
  256.6 158.8 reduce-scatter.2
  417.8 41.0 reduce-scatter.4
  464.9 253.5 all-reduce.2
where the time goes:
time: 729 us; the launch traced here: 728 us
  waiting for transfers between devices  614 us (84%)
  other arithmetic  45.3 us (6%)
  matrix products  31.8 us (4%)
  local copies, waits for them, and re-layouts  23.2 us (3%)
  between operations  13.9 us (2%)
    psum x1, waiting for transfers between devices, local(): branch_grad, trunk_grad = lax.psum((branch_grad, trunk_grad), ('fn', 'pt'))  258 us
    reduce_scatter x1, waiting for transfers between devices, local(): lax.psum_scatter(jnp.einsum('cij,cjp->ip', weight_block, trunk_val, prefe...  151 us
    all_gather x1, waiting for transfers between devices, local(): lax.all_gather(jnp.stack([latent, latent_tan]), 'pt', axis=1, tiled=True)  124 us
    reduce_scatter x1, waiting for transfers between devices, local(): lax.psum_scatter(summed * (1.0 / total_rows), 'fn', scatter_dimension=0,...  41.8 us
    all_gather x1, waiting for transfers between devices, local(): gathered = lax.all_gather(local_pair, 'fn', axis=2, tiled=True)  38.8 us
    another operation x3, other arithmetic  31.9 us
    unnamed x17, local copies, waits for them, and re-layouts  19.7 us
  transfers between devices with their start and end apart: 5, of which 5 were waited for; matrix products, arithmetic and copies ran while one was open for 5% of the time, Pallas kernels for 0%

commit v1 on v0

v1 whole, which is shorter than its diff:
```python
import functools

import jax
import jax.numpy as jnp
from jax import lax
from jax.experimental import pallas as pl
from jax.experimental.pallas import tpu as pltpu
from jax.sharding import PartitionSpec as P

F32 = jnp.float32
BF16 = jnp.bfloat16


def mm(a, b):
    return lax.dot_general(a, b, (((1,), (0,)), ((), ())), preferred_element_type=F32)


def mm_nt(a, b):
    return lax.dot_general(a, b, (((1,), (1,)), ((), ())), preferred_element_type=F32)


def mm_tn(a, b):
    return lax.dot_general(a, b, (((0,), (0,)), ((), ())), preferred_element_type=F32)


def trunk_kernel(points_ref, cols_ref, tangent_ref, out_ref, feat_ref, factor_ref):
    x, y = points_ref[0:1, :], points_ref[1:2, :]
    cx, cy, bias = cols_ref[:, 0:1], cols_ref[:, 1:2], cols_ref[:, 2:3]
    value = jnp.tanh(x * cx + y * cy + bias)
    first = 1.0 - value * value
    second = -2.0 * value * first
    feats = (second * (cx * cx + cy * cy), first * cx, first * cy)
    latent = out_ref.shape[1]
    for c in range(3):
        feat = feats[c].astype(BF16)
        feat_ref[c] = feat
        factor_ref[c, :latent, :] = mm_tn(tangent_ref[...], feat).astype(BF16)
        factor_ref[c, latent:, :] = mm_tn(out_ref[...], feat).astype(BF16)


def trunk(points, cols, trunk_tangent, trunk_out):
    width, latent = trunk_out.shape
    count = points.shape[1]
    tile = min(256, count)
    return pl.pallas_call(
        trunk_kernel,
        grid=(count // tile,),
        in_specs=[
            pl.BlockSpec((2, tile), lambda j: (0, j)),
            pl.BlockSpec((width, 3), lambda j: (0, 0)),
            pl.BlockSpec((width, latent), lambda j: (0, 0)),
            pl.BlockSpec((width, latent), lambda j: (0, 0)),
        ],
        out_specs=[
            pl.BlockSpec((3, width, tile), lambda j: (0, 0, j)),
            pl.BlockSpec((3, 2 * latent, tile), lambda j: (0, 0, j)),
        ],
        out_shape=[
            jax.ShapeDtypeStruct((3, width, count), BF16),
            jax.ShapeDtypeStruct((3, 2 * latent, count), BF16),
        ],
        cost_estimate=pl.CostEstimate(
            flops=12 * width * latent * count, bytes_accessed=12 * width * count, transcendentals=width * count
        ),
        name="trunk",
    )(points, cols, trunk_tangent, trunk_out)


def block_kernel(
    row_scale, grad_scale, col_tile, hidden_ref, slopes_ref, branch_out_ref, branch_tan_ref, factor_ref, feat_ref, out_ref, rows_ref, points_ref, branch_ref
):
    step, last = pl.program_id(0), pl.num_programs(0) - 1
    rows = hidden_ref.shape[0]
    latent = branch_out_ref.shape[1]
    count = factor_ref.shape[2]

    @pl.when(step == 0)
    def _():
        points_ref[...] = jnp.zeros_like(points_ref)
        branch_ref[...] = jnp.zeros_like(branch_ref)

    hidden = hidden_ref[...]
    lat = mm(hidden, branch_out_ref[...]).astype(BF16)
    row_factor = jnp.concatenate([lat, mm(hidden, branch_tan_ref[...]).astype(BF16)], axis=1)
    lat_t = lat.T
    total = jnp.zeros((rows, latent), F32)
    for j in range(0, count, col_tile):
        at = slice(j, j + col_tile)
        sx, sy = slopes_ref[0, :, at].astype(F32), slopes_ref[1, :, at].astype(F32)
        tangent = mm(row_factor, factor_ref[0, :, at])
        tangent = tangent + sx * mm(row_factor, factor_ref[1, :, at])
        tangent = tangent + sy * mm(row_factor, factor_ref[2, :, at])
        weights = (tangent.astype(BF16), (sx * tangent).astype(BF16), (sy * tangent).astype(BF16))
        for c in range(3):
            total = total + mm_nt(weights[c], factor_ref[c, latent:, at])
            points_ref[c, :, at] += mm(lat_t, weights[c])
    high = total.astype(BF16)
    low = (total - high.astype(F32)).astype(BF16)
    branch_ref[...] += mm_tn(hidden, high) + mm_tn(hidden, low)
    rows_ref[pl.ds(pl.multiple_of(step * rows, rows), rows), :] = (total * row_scale).astype(rows_ref.dtype)

    @pl.when(step == last)
    def _():
        members, height = out_ref.shape[0], out_ref.shape[1]
        own = rows_ref.shape[0] // members
        share = height - own
        trunk_grad = jnp.zeros((feat_ref.shape[1], latent), F32)
        for c in range(3):
            part = points_ref[c]
            high = part.astype(BF16)
            low = (part - high.astype(F32)).astype(BF16)
            trunk_grad = trunk_grad + mm_nt(feat_ref[c], high) + mm_nt(feat_ref[c], low)
        out_ref[:, :own, :] = rows_ref[...].reshape(members, own, latent)
        half = members // 2
        out_ref[:half, own:, :] = (branch_ref[...] * grad_scale).astype(out_ref.dtype).reshape(half, share, latent)
        out_ref[half:, own:, :] = (trunk_grad * grad_scale).astype(out_ref.dtype).reshape(half, share, latent)


def block(hidden, slopes, branch_out, branch_tangent, factor, feat, members, row_scale, grad_scale):
    rows, width = hidden.shape
    latent = branch_out.shape[1]
    count = slopes.shape[2]
    tile = min(256, rows)
    share = 2 * width // members
    resident = functools.partial(pl.BlockSpec, pipeline_mode=pl.Buffered(1))
    return pl.pallas_call(
        functools.partial(block_kernel, row_scale, grad_scale, min(256, count)),
        grid=(rows // tile,),
        in_specs=[
            pl.BlockSpec((tile, width), lambda i: (i, 0)),
            pl.BlockSpec((2, tile, count), lambda i: (0, i, 0)),
            resident((width, latent), lambda i: (0, 0)),
            resident((width, latent), lambda i: (0, 0)),
            resident((3, 2 * latent, count), lambda i: (0, 0, 0)),
            resident((3, feat.shape[1], count), lambda i: (0, 0, 0)),
        ],
        out_specs=pl.BlockSpec((members, rows // members + share, latent), lambda i: (0, 0, 0)),
        out_shape=jax.ShapeDtypeStruct((members, rows // members + share, latent), BF16),
        scratch_shapes=[
            pltpu.VMEM((rows, latent), BF16),
            pltpu.VMEM((3, latent, count), F32),
            pltpu.VMEM((width, latent), F32),
        ],
        cost_estimate=pl.CostEstimate(
            flops=2 * 3 * rows * count * 4 * latent, bytes_accessed=4 * rows * count, transcendentals=0
        ),
        compiler_params=pltpu.CompilerParams(vmem_limit_bytes=48 << 20),
        name="block",
    )(hidden, slopes, branch_out, branch_tangent, factor, feat)


def doubled(values, axis_name, combine):
    size = lax.axis_size(axis_name)
    me = lax.axis_index(axis_name)
    bit = 1
    while bit < size:
        other = lax.ppermute(values, axis_name, [(i, i ^ bit) for i in range(size)])
        values = combine(values, other, (me & bit) != 0)
        bit *= 2
    return values


def local(functions, branch_in, branch_out, branch_tangent, points, trunk_in, trunk_bias, trunk_out, trunk_tangent, slopes):
    members = lax.axis_size("pt")
    total_rows = functions.shape[0] * lax.axis_size("fn") * members
    total_points = points.shape[1] * lax.axis_size("fn") * members
    width = branch_in.shape[1]
    all_points = doubled(
        points,
        "fn",
        lambda mine, other, high: jnp.where(
            high, jnp.concatenate([other, mine], axis=1), jnp.concatenate([mine, other], axis=1)
        ),
    )
    hidden = jnp.tanh(jnp.dot(functions, branch_in, preferred_element_type=F32)).astype(BF16)
    own, latent = hidden.shape[0], branch_out.shape[1]
    hidden_all = lax.all_to_all(jnp.broadcast_to(hidden[None], (members,) + hidden.shape), "pt", 0, 0)
    hidden_all = hidden_all.reshape(members * own, width)
    cols = jnp.concatenate([trunk_in, trunk_bias[None]], axis=0).T
    feat, factor = trunk(all_points, cols, trunk_tangent, trunk_out)
    row_scale = 1.0 / total_points
    parts = block(
        hidden_all, slopes, branch_out, branch_tangent, factor, feat, members, row_scale, row_scale / total_rows
    )
    sums = jnp.sum(lax.all_to_all(parts, "pt", 0, 0).astype(F32), axis=0)
    row_grad = sums[:own]
    grads = doubled(sums[own:], "fn", lambda mine, other, high: mine + other)
    grads = lax.all_to_all(jnp.broadcast_to(grads[None], (members,) + grads.shape), "pt", 0, 0)
    grads = grads.reshape(2, width, latent)
    return (row_grad, grads[0], grads[1])


def solution(mesh):
    in_specs = (
        P(("fn", "pt"), None),
        P(),
        P(),
        P(),
        P(None, ("pt", "fn")),
        P(),
        P(),
        P(),
        P(),
        P(None, "fn", "pt"),
    )
    out_specs = (P(("fn", "pt"), None), P(), P())
    return jax.shard_map(local, mesh=mesh, in_specs=in_specs, out_specs=out_specs, check_vma=False)
```

time: 729 us -> 112 us (0.15)
  waiting for transfers between devices: 614 us -> 25 us
  other arithmetic: 45.3 us -> 0.73 us
  matrix products: 31.8 us -> 1.5 us
  starting transfers between devices: 0.21 us -> 28.3 us
  Pallas kernels: 0 us -> 24.7 us
  blocking collectives: 0 us -> 21.6 us
  local copies, waits for them, and re-layouts: 23.2 us -> 8.4 us
  between operations: 13.9 us -> 0.77 us
    psum x1 -> x0, waiting for transfers between devices: 258 us -> none  [local(): branch_grad, trunk_grad = lax.psum((branch_grad, trunk_grad), ('fn', 'pt'))]
    reduce_scatter x2 -> x0, waiting for transfers between devices: 193 us -> none  [the longest x1 151 us: local(): lax.psum_scatter(jnp.einsum('cij,cjp->ip', weight_block, trunk_val, prefe...]
    all_gather x2 -> x0, waiting for transfers between devices: 163 us -> none  [the longest x1 124 us: local(): lax.all_gather(jnp.stack([latent, latent_tan]), 'pt', axis=1, tiled=True)]
    another operation x5 -> x0, other arithmetic: 33.3 us -> none
    dot_general x10 -> x1, matrix products: 31.8 us -> 1.5 us  [local(): jnp.dot(functions, branch_in, preferred_element_type=F32)]
    pallas_call x0 -> x2, Pallas kernels: none -> 24.7 us  [the longest x1 20.4 us: block(): pl.pallas_call(functools.partial(block_kernel, row_scale, grad_scale, min...]
    all_to_all x0 -> x1, blocking collectives: none -> 21.6 us  [local(): sums = jnp.sum(lax.all_to_all(parts, 'pt', 0, 0).astype(F32), axis=0)]
    ppermute x0 -> x6, waiting for transfers between devices: none -> 17.3 us  [doubled(): other = lax.ppermute(values, axis_name, [(i, i ^ bit) for i in range(size)])]
  transfers between devices with their start and end apart: 5 -> 8, of which waited for: 5 -> 7; matrix products, arithmetic and copies ran while one was open for 5% -> 2% of each run, Pallas kernels for 0% -> 4%
where the time goes in v1:
time: 112 us; the launch traced here: 111 us
  starting transfers between devices  28.3 us (25%)
  waiting for transfers between devices  25 us (22%)
  Pallas kernels  24.7 us (22%)
  blocking collectives  21.6 us (19%)
  local copies, waits for them, and re-layouts  8.4 us (8%)
  matrix products  1.5 us (1%)
    all_to_all x1, blocking collectives, local(): sums = jnp.sum(lax.all_to_all(parts, 'pt', 0, 0).astype(F32), axis=0)  21.6 us
    pallas_call x1, Pallas kernels, block(): pl.pallas_call(functools.partial(block_kernel, row_scale, grad_scale, min...  20.4 us
    ppermute x6, waiting for transfers between devices, doubled(): other = lax.ppermute(values, axis_name, [(i, i ^ bit) for i in range(size)])  17.3 us
    ppermute x6, starting transfers between devices, doubled(): other = lax.ppermute(values, axis_name, [(i, i ^ bit) for i in range(size)])  14.3 us
    all_to_all x1, starting transfers between devices, local(): lax.all_to_all(jnp.broadcast_to(hidden[None], (members,) + hidden.shape),...  9.02 us
    all_to_all x1, waiting for transfers between devices, local(): lax.all_to_all(jnp.broadcast_to(grads[None], (members,) + grads.shape), '...  7.72 us
    all_to_all x1, starting transfers between devices, local(): lax.all_to_all(jnp.broadcast_to(grads[None], (members,) + grads.shape), '...  5.02 us
    unnamed x16, local copies, waits for them, and re-layouts  4.42 us
  transfers between devices with their start and end apart: 8, of which 7 were waited for; matrix products, arithmetic and copies ran while one was open for 2% of the time, Pallas kernels for 4%

profile of v1, /device:TPU:8, one launch (start us, length us, event | category | flops | bytes accessed | tf_op | source)
XLA Modules:
  0.0 111.1 jit_solution(5051433071467170002)
XLA Ops:
  0.6 0.0 copy-start
  0.6 1.6 %copy-done = bf16[4096,256]{1,0:T(8,128)(2,1)S(1)} copy-done((bf16[4096,256]{1,0:T(8,128)(2,1)S(1)}, bf16[4096,256]{1,0:T(8,128)(2,1)}, u32[]{:S(2)}) %copy-start) | copy-done | bytes 2097176
  2.2 1.5 %fusion = bf16[64,256]{1,0:T(8,128)(2,1)S(1)} fusion(bf16[64,4096]{1,0:T(8,128)(2,1)} %param.10, bf16[4096,256]{1,0:T(8,128)(2,1)S(1)} %copy-done), kind=kOutput, calls=%fused_computation.2 | convolution fusion | flops 134234112 | bytes 2654208 | tf_op jit(solution)/shard_map/dot_general | solution.py:175
  3.7 0.0 copy-start.7
  3.8 0.0 copy-start.5
  3.8 0.0 copy-start.6
  3.8 1.1 %broadcast_in_dim.6 = bf16[32,64,256]{2,1,0:T(8,128)(2,1)} broadcast(bf16[64,256]{1,0:T(8,128)(2,1)S(1)} %fusion), dimensions={1,2} | broadcast | bytes 1081344 | tf_op jit(solution)/shard_map/broadcast_in_dim | solution.py:177
  4.9 0.0 copy-start.1
  4.9 0.0 copy-start.2
  4.9 9.0 %all-to-all-start = ((bf16[32,64,256]{2,1,0:T(8,128)(2,1)}), bf16[32,64,256]{2,1,0:T(8,128)(2,1)S(1)}, u32[]{:S(2)}, u32[]{:S(2)}) async-start(bf16[32,64,256]{2,1,0:T(8,128)(2,1)} %broadcast_in_dim.6), calls=%async_computation | async-start | bytes 2097152 | tf_op jit(solution)/shard_map/all_to_all | solution.py:177
  13.9 0.0 copy-done.7
  13.9 0.1 collective-permute-start
  14.1 1.1 %collective-permute-done = f32[2,128]{1,0:T(2,128)S(1)} collective-permute-done((f32[2,128]{1,0:T(2,128)S(1)}, f32[2,128]{1,0:T(2,128)S(1)}, u32[]{:S(2)}, u32[]{:S(2)}) %collective-permute-start) | collective-permute-done | bytes 1056 | tf_op jit(solution)/shard_map/ppermute | solution.py:157
  15.2 3.3 %collective-permute-start.1 = (f32[2,256]{1,0:T(2,128)S(1)}, f32[2,256]{1,0:T(2,128)S(1)}, u32[]{:S(2)}, u32[]{:S(2)}) collective-permute-start(f32[2,256]{1,0:T(2,128)S(1)} %maximum_select_fusion.2), channel_id=1, source_target_pairs={{0,64},{32,96},{64,0},{96,32},{128,192},{160,224},{192,128},{224,1... | collective-permute-start | bytes 6152 | tf_op jit(solution)/shard_map/ppermute | solution.py:157
  18.5 6.6 %collective-permute-done.1 = f32[2,256]{1,0:T(2,128)S(1)} collective-permute-done((f32[2,256]{1,0:T(2,128)S(1)}, f32[2,256]{1,0:T(2,128)S(1)}, u32[]{:S(2)}, u32[]{:S(2)}) %collective-permute-start.1) | collective-permute-done | bytes 2080 | tf_op jit(solution)/shard_map/ppermute | solution.py:157
  25.1 6.3 %collective-permute-start.2 = (f32[2,512]{1,0:T(2,128)S(1)}, f32[2,512]{1,0:T(2,128)S(1)}, u32[]{:S(2)}, u32[]{:S(2)}) collective-permute-start(f32[2,512]{1,0:T(2,128)S(1)} %maximum_select_fusion.1), channel_id=1, source_target_pairs={{0,128},{32,160},{64,192},{96,224},{128,0},{160,32},{192,64},{224,... | collective-permute-start | bytes 12296 | tf_op jit(solution)/shard_map/ppermute | solution.py:157
  31.5 0.0 copy-done.5
  31.5 0.0 copy-done.6
  31.5 0.8 copy.16
  32.3 0.8 collective-permute-done.2
  33.0 0.6 maximum_select_fusion.points_ref
  33.6 4.3 %trunk.1 = (bf16[3,256,1024]{2,1,0:T(8,128)(2,1)}, bf16[3,256,1024]{2,1,0:T(8,128)(2,1)}) custom-call(f32[2,1024]{1,0:T(2,128)} %maximum_select_fusion.points_ref, f32[256,3]{1,0:T(8,128)} %bitcast.8, bf16[256,128]{1,0:T(8,128)(2,1)} %tangent_ref.1, bf16[256,128]{1,0:T(8,128)(2,1)} %out_ref.1), custom_call_target="tpu_custom_call" | custom-call | flops 402653184 | bytes 3145728 | tf_op jit(solution)/shard_map/trunk/pallas_call | solution.py:45
  38.0 0.0 all-to-all-done
  38.0 0.0 copy-done.1
  38.0 0.0 copy-done.2
  38.0 0.0 copy-start.3
  38.0 1.4 %copy-done.3 = bf16[3,256,1024]{2,1,0:T(8,128)(2,1)S(1)} copy-done((bf16[3,256,1024]{2,1,0:T(8,128)(2,1)S(1)}, bf16[3,256,1024]{2,1,0:T(8,128)(2,1)}, u32[]{:S(2)}) %copy-start.3) | copy-done | bytes 1572888
  39.4 0.0 copy-start.4
  39.4 1.4 %copy-done.4 = bf16[3,256,1024]{2,1,0:T(8,128)(2,1)S(1)} copy-done((bf16[3,256,1024]{2,1,0:T(8,128)(2,1)S(1)}, bf16[3,256,1024]{2,1,0:T(8,128)(2,1)}, u32[]{:S(2)}) %copy-start.4) | copy-done | bytes 1572888
  40.8 20.4 %block.1 = bf16[32,80,128]{2,1,0:T(8,128)(2,1)S(1)} custom-call(bf16[2048,256]{1,0:T(8,128)(2,1)S(1)} %bitcast.7, bf16[2,2048,1024]{2,1,0:T(8,128)(2,1)} %slopes_ref.1, bf16[256,128]{1,0:T(8,128)(2,1)S(1)} %copy-done.1, bf16[256,128]{1,0:T(8,128)(2,1)S(1)} %copy-done.2, bf16[3,256,1024]{2,1,0:T(8,128)(2,1)S(1)} %copy-done.4, bf16[3,256,1024]{2,1,0:T(8,128)(2,1)S(1)} %copy-done.3), custom_call_target="tpu_custom_call" | custom-call | flops 6442450944 | bytes 8388608 | tf_op jit(solution)/shard_map/block/pallas_call | solution.py:126
  61.2 21.6 %all_to_all.15 = bf16[32,80,128]{2,1,0:T(8,128)(2,1)S(1)} all-to-all(bf16[32,80,128]{2,1,0:T(8,128)(2,1)S(1)} %block.1), channel_id=1, replica_groups=mesh['fn'=8,'pt'=32] {'pt'}, dimensions={0} | all-to-all | bytes 1310720 | tf_op jit(solution)/shard_map/all_to_all | solution.py:185
  82.8 0.1 convert_reduce_fusion
  82.9 0.1 collective-permute-start.3
  83.0 1.2 %collective-permute-done.3 = f32[16,128]{1,0:T(8,128)S(1)} collective-permute-done((f32[16,128]{1,0:T(8,128)S(1)}, f32[16,128]{1,0:T(8,128)S(1)}, u32[]{:S(2)}, u32[]{:S(2)}) %collective-permute-start.3) | collective-permute-done | bytes 8224 | tf_op jit(solution)/shard_map/ppermute | solution.py:157
  84.2 0.0 collective-permute-start.4
  84.2 4.5 %collective-permute-done.4 = f32[16,128]{1,0:T(8,128)S(1)} collective-permute-done((f32[16,128]{1,0:T(8,128)S(1)}, f32[16,128]{1,0:T(8,128)S(1)}, u32[]{:S(2)}, u32[]{:S(2)}) %collective-permute-start.4) | collective-permute-done | bytes 8224 | tf_op jit(solution)/shard_map/ppermute | solution.py:157
  88.7 4.5 %collective-permute-start.5 = (f32[16,128]{1,0:T(8,128)S(1)}, f32[16,128]{1,0:T(8,128)S(1)}, u32[]{:S(2)}, u32[]{:S(2)}) collective-permute-start(f32[16,128]{1,0:T(8,128)S(1)} %add.10), channel_id=1, source_target_pairs={{0,128},{32,160},{64,192},{96,224},{128,0},{160,32},{192,64},{224,... | collective-permute-start | bytes 24584 | tf_op jit(solution)/shard_map/ppermute | solution.py:157
  93.2 3.1 %collective-permute-done.5 = f32[16,128]{1,0:T(8,128)S(1)} collective-permute-done((f32[16,128]{1,0:T(8,128)S(1)}, f32[16,128]{1,0:T(8,128)S(1)}, u32[]{:S(2)}, u32[]{:S(2)}) %collective-permute-start.5) | collective-permute-done | bytes 8224 | tf_op jit(solution)/shard_map/ppermute | solution.py:157
  96.3 0.7 broadcast_in_dim.8
  97.0 5.0 %all-to-all-start.2 = ((f32[32,16,128]{2,1,0:T(8,128)}), f32[32,16,128]{2,1,0:T(8,128)S(1)}, u32[]{:S(2)}, u32[]{:S(2)}) async-start(f32[32,16,128]{2,1,0:T(8,128)} %broadcast_in_dim.8), calls=%async_computation.2 | async-start | bytes 524288 | tf_op jit(solution)/shard_map/all_to_all | solution.py:188
  102.0 0.6 slice.18
  102.7 7.7 %all-to-all-done.2 = f32[32,16,128]{2,1,0:T(8,128)S(1)} async-done(((f32[32,16,128]{2,1,0:T(8,128)}), f32[32,16,128]{2,1,0:T(8,128)S(1)}, u32[]{:S(2)}, u32[]{:S(2)}) %all-to-all-start.2) | async-done | bytes 262176 | tf_op jit(solution)/shard_map/all_to_all | solution.py:188
  110.4 0.7 fusion.1
  (7 shorter events, 0.0 us)
Async XLA Ops:
  0.6 1.6 %copy-start = (bf16[4096,256]{1,0:T(8,128)(2,1)S(1)}, bf16[4096,256]{1,0:T(8,128)(2,1)}, u32[]{:S(2)}) copy-start(bf16[4096,256]{1,0:T(8,128)(2,1)} %param.11) | copy-start | bytes 6291460
  3.7 10.2 %copy-start.7 = (f32[2,128]{1,0:T(2,128)S(1)}, f32[2,128]{1,0:T(2,128)}, u32[]{:S(2)}) copy-start(f32[2,128]{1,0:T(2,128)} %param.14) | copy-start | bytes 3076
  3.8 27.7 %copy-start.5 = (f32[2,256]{1,0:T(2,128)S(1)}, f32[2,256]{1,0:T(2,128)}, u32[]{:S(2)}) copy-start(f32[2,256]{1,0:T(2,128)} %param.15) | copy-start | bytes 6148
  3.8 27.7 %copy-start.6 = (f32[256]{0:T(256)S(1)}, f32[256]{0:T(256)}, u32[]{:S(2)}) copy-start(f32[256]{0:T(256)} %param.16) | copy-start | bytes 3076
  4.9 33.1 %copy-start.1 = (bf16[256,128]{1,0:T(8,128)(2,1)S(1)}, bf16[256,128]{1,0:T(8,128)(2,1)}, u32[]{:S(2)}) copy-start(bf16[256,128]{1,0:T(8,128)(2,1)} %branch_out_ref.1) | copy-start | bytes 196612
  4.9 33.1 %copy-start.2 = (bf16[256,128]{1,0:T(8,128)(2,1)S(1)}, bf16[256,128]{1,0:T(8,128)(2,1)}, u32[]{:S(2)}) copy-start(bf16[256,128]{1,0:T(8,128)(2,1)} %branch_tan_ref.1) | copy-start | bytes 196612
  4.9 33.1 %all-to-all-start = ((bf16[32,64,256]{2,1,0:T(8,128)(2,1)}), bf16[32,64,256]{2,1,0:T(8,128)(2,1)S(1)}, u32[]{:S(2)}, u32[]{:S(2)}) async-start(bf16[32,64,256]{2,1,0:T(8,128)(2,1)} %broadcast_in_dim.6), calls=%async_computation | async-start | bytes 2097152 | tf_op jit(solution)/shard_map/all_to_all | solution.py:177
  13.9 1.2 %collective-permute-start = (f32[2,128]{1,0:T(2,128)S(1)}, f32[2,128]{1,0:T(2,128)S(1)}, u32[]{:S(2)}, u32[]{:S(2)}) collective-permute-start(f32[2,128]{1,0:T(2,128)S(1)} %copy-done.7), channel_id=1, source_target_pairs={{0,32},{32,0},{64,96},{96,64},{128,160},{160,128},{192,224},{224,1... | collective-permute-start | bytes 3080 | tf_op jit(solution)/shard_map/ppermute | solution.py:157
  15.2 9.9 %collective-permute-start.1 = (f32[2,256]{1,0:T(2,128)S(1)}, f32[2,256]{1,0:T(2,128)S(1)}, u32[]{:S(2)}, u32[]{:S(2)}) collective-permute-start(f32[2,256]{1,0:T(2,128)S(1)} %maximum_select_fusion.2), channel_id=1, source_target_pairs={{0,64},{32,96},{64,0},{96,32},{128,192},{160,224},{192,128},{224,1... | collective-permute-start | bytes 6152 | tf_op jit(solution)/shard_map/ppermute | solution.py:157
  25.1 7.9 %collective-permute-start.2 = (f32[2,512]{1,0:T(2,128)S(1)}, f32[2,512]{1,0:T(2,128)S(1)}, u32[]{:S(2)}, u32[]{:S(2)}) collective-permute-start(f32[2,512]{1,0:T(2,128)S(1)} %maximum_select_fusion.1), channel_id=1, source_target_pairs={{0,128},{32,160},{64,192},{96,224},{128,0},{160,32},{192,64},{224,... | collective-permute-start | bytes 12296 | tf_op jit(solution)/shard_map/ppermute | solution.py:157
  38.0 1.4 %copy-start.3 = (bf16[3,256,1024]{2,1,0:T(8,128)(2,1)S(1)}, bf16[3,256,1024]{2,1,0:T(8,128)(2,1)}, u32[]{:S(2)}) copy-start(bf16[3,256,1024]{2,1,0:T(8,128)(2,1)} %get-tuple-element.6.feat_ref) | copy-start | bytes 4718596
  39.4 1.4 %copy-start.4 = (bf16[3,256,1024]{2,1,0:T(8,128)(2,1)S(1)}, bf16[3,256,1024]{2,1,0:T(8,128)(2,1)}, u32[]{:S(2)}) copy-start(bf16[3,256,1024]{2,1,0:T(8,128)(2,1)} %get-tuple-element.5.factor_ref) | copy-start | bytes 4718596
  82.9 1.3 %collective-permute-start.3 = (f32[16,128]{1,0:T(8,128)S(1)}, f32[16,128]{1,0:T(8,128)S(1)}, u32[]{:S(2)}, u32[]{:S(2)}) collective-permute-start(f32[16,128]{1,0:T(8,128)S(1)} %slice.19), channel_id=1, source_target_pairs={{0,32},{32,0},{64,96},{96,64},{128,160},{160,128},{192,224},{224,1... | collective-permute-start | bytes 24584 | tf_op jit(solution)/shard_map/ppermute | solution.py:157
  84.2 4.5 %collective-permute-start.4 = (f32[16,128]{1,0:T(8,128)S(1)}, f32[16,128]{1,0:T(8,128)S(1)}, u32[]{:S(2)}, u32[]{:S(2)}) collective-permute-start(f32[16,128]{1,0:T(8,128)S(1)} %slice_add_fusion), channel_id=1, source_target_pairs={{0,64},{32,96},{64,0},{96,32},{128,192},{160,224},{192,128},{224,1... | collective-permute-start | bytes 24584 | tf_op jit(solution)/shard_map/ppermute | solution.py:157
  88.7 7.6 %collective-permute-start.5 = (f32[16,128]{1,0:T(8,128)S(1)}, f32[16,128]{1,0:T(8,128)S(1)}, u32[]{:S(2)}, u32[]{:S(2)}) collective-permute-start(f32[16,128]{1,0:T(8,128)S(1)} %add.10), channel_id=1, source_target_pairs={{0,128},{32,160},{64,192},{96,224},{128,0},{160,32},{192,64},{224,... | collective-permute-start | bytes 24584 | tf_op jit(solution)/shard_map/ppermute | solution.py:157
  97.0 13.4 %all-to-all-start.2 = ((f32[32,16,128]{2,1,0:T(8,128)}), f32[32,16,128]{2,1,0:T(8,128)S(1)}, u32[]{:S(2)}, u32[]{:S(2)}) async-start(f32[32,16,128]{2,1,0:T(8,128)} %broadcast_in_dim.8), calls=%async_computation.2 | async-start | bytes 524288 | tf_op jit(solution)/shard_map/all_to_all | solution.py:188

commit v2 on v1

v2 whole, which is shorter than its diff:
```python
import functools

import jax
import jax.numpy as jnp
from jax import lax
from jax.experimental import pallas as pl
from jax.experimental.pallas import tpu as pltpu
from jax.sharding import PartitionSpec as P

F32 = jnp.float32
BF16 = jnp.bfloat16


def mm(a, b):
    return lax.dot_general(a, b, (((1,), (0,)), ((), ())), preferred_element_type=F32)


def mm_nt(a, b):
    return lax.dot_general(a, b, (((1,), (1,)), ((), ())), preferred_element_type=F32)


def mm_tn(a, b):
    return lax.dot_general(a, b, (((0,), (0,)), ((), ())), preferred_element_type=F32)


def trunk(points_ref, cols_ref, tangent_ref, out_ref, feat_ref, factor_ref, col_tile):
    cx, cy, bias = cols_ref[:, 0:1], cols_ref[:, 1:2], cols_ref[:, 2:3]
    square = cx * cx + cy * cy
    latent = out_ref.shape[1]
    for j in range(0, points_ref.shape[1], col_tile):
        at = slice(j, j + col_tile)
        value = jnp.tanh(points_ref[0:1, at] * cx + points_ref[1:2, at] * cy + bias)
        first = 1.0 - value * value
        second = -2.0 * value * first
        for c, feat in enumerate((second * square, first * cx, first * cy)):
            feat = feat.astype(BF16)
            feat_ref[c, :, at] = feat
            factor_ref[c, :latent, at] = mm_tn(tangent_ref[...], feat).astype(BF16)
            factor_ref[c, latent:, at] = mm_tn(out_ref[...], feat).astype(BF16)


def block_kernel(
    row_scale,
    grad_scale,
    col_tile,
    hidden_ref,
    slopes_ref,
    branch_out_ref,
    branch_tan_ref,
    at_ref,
    cols_ref,
    trunk_out_ref,
    trunk_tan_ref,
    out_ref,
    rows_ref,
    points_ref,
    branch_ref,
    feat_ref,
    factor_ref,
):
    step, last = pl.program_id(0), pl.num_programs(0) - 1
    rows = hidden_ref.shape[0]
    latent = branch_out_ref.shape[1]
    count = factor_ref.shape[2]

    @pl.when(step == 0)
    def _():
        points_ref[...] = jnp.zeros_like(points_ref)
        branch_ref[...] = jnp.zeros_like(branch_ref)
        trunk(at_ref, cols_ref, trunk_tan_ref, trunk_out_ref, feat_ref, factor_ref, col_tile)

    hidden = hidden_ref[...]
    lat = mm(hidden, branch_out_ref[...]).astype(BF16)
    row_factor = jnp.concatenate([lat, mm(hidden, branch_tan_ref[...]).astype(BF16)], axis=1)
    lat_t = lat.T
    total = jnp.zeros((rows, latent), F32)
    for j in range(0, count, col_tile):
        at = slice(j, j + col_tile)
        sx, sy = slopes_ref[0, :, at].astype(F32), slopes_ref[1, :, at].astype(F32)
        tangent = mm(row_factor, factor_ref[0, :, at])
        tangent = tangent + sx * mm(row_factor, factor_ref[1, :, at])
        tangent = tangent + sy * mm(row_factor, factor_ref[2, :, at])
        weights = (tangent.astype(BF16), (sx * tangent).astype(BF16), (sy * tangent).astype(BF16))
        for c in range(3):
            total = total + mm_nt(weights[c], factor_ref[c, latent:, at])
            points_ref[c, :, at] += mm(lat_t, weights[c])
    high = total.astype(BF16)
    low = (total - high.astype(F32)).astype(BF16)
    branch_ref[...] += mm_tn(hidden, high) + mm_tn(hidden, low)
    rows_ref[pl.ds(pl.multiple_of(step * rows, rows), rows), :] = (total * row_scale).astype(rows_ref.dtype)

    @pl.when(step == last)
    def _():
        members, height = out_ref.shape[0], out_ref.shape[1]
        own = rows_ref.shape[0] // members
        share = height - own
        trunk_grad = jnp.zeros((feat_ref.shape[1], latent), F32)
        for c in range(3):
            part = points_ref[c]
            high = part.astype(BF16)
            low = (part - high.astype(F32)).astype(BF16)
            trunk_grad = trunk_grad + mm_nt(feat_ref[c], high) + mm_nt(feat_ref[c], low)
        out_ref[:, :own, :] = rows_ref[...].reshape(members, own, latent)
        half = members // 2
        out_ref[:half, own:, :] = (branch_ref[...] * grad_scale).astype(out_ref.dtype).reshape(half, share, latent)
        out_ref[half:, own:, :] = (trunk_grad * grad_scale).astype(out_ref.dtype).reshape(half, share, latent)


def block(hidden, slopes, branch_out, branch_tangent, points, cols, trunk_out, trunk_tangent, members, row_scale, grad_scale):
    rows, width = hidden.shape
    latent = branch_out.shape[1]
    count = slopes.shape[2]
    tile = min(512, rows)
    share = 2 * width // members
    resident = functools.partial(pl.BlockSpec, pipeline_mode=pl.Buffered(1))
    return pl.pallas_call(
        functools.partial(block_kernel, row_scale, grad_scale, min(256, count)),
        grid=(rows // tile,),
        in_specs=[
            pl.BlockSpec((tile, width), lambda i: (i, 0)),
            pl.BlockSpec((2, tile, count), lambda i: (0, i, 0)),
            resident((width, latent), lambda i: (0, 0)),
            resident((width, latent), lambda i: (0, 0)),
            resident(points.shape, lambda i: (0, 0)),
            resident(cols.shape, lambda i: (0, 0)),
            resident(trunk_out.shape, lambda i: (0, 0)),
            resident(trunk_out.shape, lambda i: (0, 0)),
        ],
        out_specs=pl.BlockSpec((members, rows // members + share, latent), lambda i: (0, 0, 0)),
        out_shape=jax.ShapeDtypeStruct((members, rows // members + share, latent), BF16),
        scratch_shapes=[
            pltpu.VMEM((rows, latent), BF16),
            pltpu.VMEM((3, latent, count), F32),
            pltpu.VMEM((width, latent), F32),
            pltpu.VMEM((3, trunk_out.shape[0], count), BF16),
            pltpu.VMEM((3, 2 * latent, count), BF16),
        ],
        cost_estimate=pl.CostEstimate(
            flops=2 * 3 * rows * count * 4 * latent, bytes_accessed=4 * rows * count, transcendentals=0
        ),
        compiler_params=pltpu.CompilerParams(vmem_limit_bytes=48 << 20),
        name="block",
    )(hidden, slopes, branch_out, branch_tangent, points, cols, trunk_out, trunk_tangent)


def points_of(points, mask):
    return lax.ppermute(points, "fn", [(i, i ^ mask) for i in range(lax.axis_size("fn"))])


def joined(mine, other, high):
    return jnp.where(high != 0, jnp.concatenate([other, mine], axis=1), jnp.concatenate([mine, other], axis=1))


def summed(values):
    size = lax.axis_size("fn")
    values = values + lax.ppermute(values, "fn", [(i, i ^ 1) for i in range(size)])
    ahead = [(i, (i + 2) % size) for i in range(size)]
    behind = lax.ppermute(values, "fn", ahead)
    opposite = lax.ppermute(behind, "fn", ahead)
    front = lax.ppermute(values, "fn", [(b, a) for a, b in ahead])
    return (values + opposite) + (behind + front)


def local(functions, branch_in, branch_out, branch_tangent, points, trunk_in, trunk_bias, trunk_out, trunk_tangent, slopes):
    members = lax.axis_size("pt")
    total_rows = functions.shape[0] * lax.axis_size("fn") * members
    total_points = points.shape[1] * lax.axis_size("fn") * members
    width = branch_in.shape[1]
    column = lax.axis_index("fn")
    first = joined(points, points_of(points, 1), column & 1)
    hidden = jnp.tanh(jnp.dot(functions, branch_in, preferred_element_type=F32)).astype(BF16)
    second = joined(first, points_of(first, 2), column & 2)
    own, latent = hidden.shape[0], branch_out.shape[1]
    copies, second = lax.optimization_barrier((jnp.broadcast_to(hidden[None], (members,) + hidden.shape), second))
    hidden_all = lax.all_to_all(copies, "pt", 0, 0)
    hidden_all = hidden_all.reshape(members * own, width)
    all_points = joined(second, points_of(second, 4), column & 4)
    cols = jnp.concatenate([trunk_in, trunk_bias[None]], axis=0).T
    row_scale = 1.0 / total_points
    parts = block(
        hidden_all,
        slopes,
        branch_out,
        branch_tangent,
        all_points,
        cols,
        trunk_out,
        trunk_tangent,
        members,
        row_scale,
        row_scale / total_rows,
    )
    sums = jnp.sum(lax.all_to_all(parts, "pt", 0, 0).astype(F32), axis=0)
    row_grad = sums[:own]
    grads = summed(sums[own:])
    grads = lax.all_to_all(jnp.broadcast_to(grads[None], (members,) + grads.shape), "pt", 0, 0)
    grads = grads.reshape(2, width, latent)
    return (row_grad, grads[0], grads[1])


def solution(mesh):
    in_specs = (
        P(("fn", "pt"), None),
        P(),
        P(),
        P(),
        P(None, ("pt", "fn")),
        P(),
        P(),
        P(),
        P(),
        P(None, "fn", "pt"),
    )
    out_specs = (P(("fn", "pt"), None), P(), P())
    return jax.shard_map(local, mesh=mesh, in_specs=in_specs, out_specs=out_specs, check_vma=False)
```

time: 112 us -> 97.8 us (0.87)
  Pallas kernels: 24.7 us -> 17 us
  local copies, waits for them, and re-layouts: 8.4 us -> 3.33 us
  blocking collectives: 21.6 us -> 18.2 us
  waiting for transfers between devices: 25 us -> 28.1 us
    unnamed x16 -> x14, local copies, waits for them, and re-layouts: 4.42 us -> 0.05 us
    pallas_call x1 -> x0, Pallas kernels: 4.35 us -> none  [trunk(): pl.pallas_call(trunk_kernel, grid=(count // tile,), in_specs=[pl.BlockSpe...]
    pallas_call x1, Pallas kernels: 20.4 us -> 17 us  [block(): pl.pallas_call(functools.partial(block_kernel, row_scale, grad_scale, min...]
    all_to_all x1, blocking collectives: 21.6 us -> 18.2 us  [local(): sums = jnp.sum(lax.all_to_all(parts, 'pt', 0, 0).astype(F32), axis=0)]
    ppermute x6 -> x7, waiting for transfers between devices: 17.3 us -> 20.1 us  [the longest x3 11.9 us: points_of(): lax.ppermute(points, 'fn', [(i, i ^ mask) for i in range(lax.axis_size('f...]
    ppermute x6 -> x7, starting transfers between devices: 14.3 us -> 13.9 us  [the longest x3 9.34 us: points_of(): lax.ppermute(points, 'fn', [(i, i ^ mask) for i in range(lax.axis_size('f...]
  transfers between devices with their start and end apart: 8 -> 9, of which waited for: 7 -> 7; matrix products, arithmetic and copies ran while one was open for 2% -> 2% of each run, Pallas kernels for 4% -> 0%
where the time goes in v2:
time: 97.8 us; the launch traced here: 97.5 us
  waiting for transfers between devices  28.1 us (29%)
  starting transfers between devices  27.7 us (28%)
  blocking collectives  18.2 us (19%)
  Pallas kernels  17 us (17%)
  local copies, waits for them, and re-layouts  3.33 us (3%)
  matrix products  1.5 us (2%)
    all_to_all x1, blocking collectives, local(): sums = jnp.sum(lax.all_to_all(parts, 'pt', 0, 0).astype(F32), axis=0)  18.2 us
    pallas_call x1, Pallas kernels, block(): pl.pallas_call(functools.partial(block_kernel, row_scale, grad_scale, min...  17 us
    ppermute x3, waiting for transfers between devices, points_of(): lax.ppermute(points, 'fn', [(i, i ^ mask) for i in range(lax.axis_size('f...  11.9 us
    ppermute x3, starting transfers between devices, points_of(): lax.ppermute(points, 'fn', [(i, i ^ mask) for i in range(lax.axis_size('f...  9.34 us
    all_to_all x1, starting transfers between devices, local(): hidden_all = lax.all_to_all(copies, 'pt', 0, 0)  8.89 us
    all_to_all x1, waiting for transfers between devices, local(): lax.all_to_all(jnp.broadcast_to(grads[None], (members,) + grads.shape), '...  7.72 us
    ppermute x1, waiting for transfers between devices, summed(): opposite = lax.ppermute(behind, 'fn', ahead)  5.46 us
    all_to_all x1, starting transfers between devices, local(): lax.all_to_all(jnp.broadcast_to(grads[None], (members,) + grads.shape), '...  4.98 us
  transfers between devices with their start and end apart: 9, of which 7 were waited for; matrix products, arithmetic and copies ran while one was open for 2% of the time, Pallas kernels for 0%

profile of v2, /device:TPU:8, one launch (start us, length us, event | category | flops | bytes accessed | tf_op | source)
XLA Modules:
  0.0 97.5 jit_solution(1494443152676227766)
XLA Ops:
  0.6 0.0 copy-start
  0.6 0.1 collective-permute-start
  0.8 1.4 %collective-permute-done = f32[2,128]{1,0:T(2,128)S(1)} collective-permute-done((f32[2,128]{1,0:T(2,128)}, f32[2,128]{1,0:T(2,128)S(1)}, u32[]{:S(2)}, u32[]{:S(2)}) %collective-permute-start) | collective-permute-done | bytes 1056 | tf_op jit(solution)/shard_map/ppermute | solution.py:147
  2.1 0.8 maximum_select_fusion.2
  2.9 3.3 %collective-permute-start.1 = (f32[2,256]{1,0:T(2,128)S(1)}, f32[2,256]{1,0:T(2,128)S(1)}, u32[]{:S(2)}, u32[]{:S(2)}) collective-permute-start(f32[2,256]{1,0:T(2,128)S(1)} %maximum_select_fusion.2), channel_id=1, source_target_pairs={{0,64},{32,96},{64,0},{96,32},{128,192},{160,224},{192,128},{224,1... | collective-permute-start | bytes 6152 | tf_op jit(solution)/shard_map/ppermute | solution.py:147
  6.1 0.0 copy-done
  6.1 1.5 %fusion = bf16[64,256]{1,0:T(8,128)(2,1)S(1)} fusion(bf16[64,4096]{1,0:T(8,128)(2,1)} %param.10, bf16[4096,256]{1,0:T(8,128)(2,1)S(1)} %copy-done), kind=kOutput, calls=%fused_computation.2 | convolution fusion | flops 134234112 | bytes 2654208 | tf_op jit(solution)/shard_map/dot_general | solution.py:171
  7.7 0.0 copy-start.5
  7.7 0.0 copy-start.6
  7.7 0.0 copy-start.1
  7.7 0.0 copy-start.2
  7.7 0.0 copy-start.3
  7.7 0.0 copy-start.4
  7.7 0.0 collective-permute-done.1
  7.8 1.1 %broadcast_in_dim.6 = bf16[32,64,256]{2,1,0:T(8,128)(2,1)} broadcast(bf16[64,256]{1,0:T(8,128)(2,1)S(1)} %fusion), dimensions={1,2} | broadcast | bytes 1081344 | tf_op jit(solution)/shard_map/broadcast_in_dim | solution.py:174
  8.8 8.9 %all-to-all-start = ((bf16[32,64,256]{2,1,0:T(8,128)(2,1)}), bf16[32,64,256]{2,1,0:T(8,128)(2,1)S(1)}, u32[]{:S(2)}, u32[]{:S(2)}) async-start(bf16[32,64,256]{2,1,0:T(8,128)(2,1)} %broadcast_in_dim.6), calls=%async_computation | async-start | bytes 2097152 | tf_op jit(solution)/shard_map/all_to_all | solution.py:175
  17.7 6.0 %collective-permute-start.2 = (f32[2,512]{1,0:T(2,128)S(1)}, f32[2,512]{1,0:T(2,128)S(1)}, u32[]{:S(2)}, u32[]{:S(2)}) collective-permute-start(f32[2,512]{1,0:T(2,128)S(1)} %maximum_select_fusion.1), channel_id=1, source_target_pairs={{0,128},{32,160},{64,192},{96,224},{128,0},{160,32},{192,64},{224,... | collective-permute-start | bytes 12296 | tf_op jit(solution)/shard_map/ppermute | solution.py:147
  23.7 0.0 copy-done.5
  23.7 0.0 copy-done.6
  23.7 0.1 copy.16
  23.9 10.5 %collective-permute-done.2 = f32[2,512]{1,0:T(2,128)S(1)} collective-permute-done((f32[2,512]{1,0:T(2,128)S(1)}, f32[2,512]{1,0:T(2,128)S(1)}, u32[]{:S(2)}, u32[]{:S(2)}) %collective-permute-start.2) | collective-permute-done | bytes 4128 | tf_op jit(solution)/shard_map/ppermute | solution.py:147
  34.4 0.2 all-to-all-done
  34.6 0.0 copy-done.1
  34.6 0.0 copy-done.2
  34.6 0.0 copy-done.3
  34.7 0.0 copy-done.4
  34.7 17.0 %block.1 = bf16[32,80,128]{2,1,0:T(8,128)(2,1)S(1)} custom-call(bf16[2048,256]{1,0:T(8,128)(2,1)S(1)} %bitcast.7, bf16[2,2048,1024]{2,1,0:T(8,128)(2,1)} %slopes_ref.1, bf16[256,128]{1,0:T(8,128)(2,1)S(1)} %copy-done.1, bf16[256,128]{1,0:T(8,128)(2,1)S(1)} %copy-done.2, f32[2,1024]{1,0:T(2,128)S(1)} %maximum_select_fusion.at_ref, f32[256,3]{1,0:T(8,128)S(1)} %bitcast.8, ...), custom_call_target="tpu_custom_call" | custom-call | flops 6442450944 | bytes 8388608 | tf_op jit(solution)/shard_map/block/pallas_call | solution.py:116
  51.6 18.2 %all_to_all.15 = bf16[32,80,128]{2,1,0:T(8,128)(2,1)S(1)} all-to-all(bf16[32,80,128]{2,1,0:T(8,128)(2,1)S(1)} %block.1), channel_id=1, replica_groups=mesh['fn'=8,'pt'=32] {'pt'}, dimensions={0} | all-to-all | bytes 1310720 | tf_op jit(solution)/shard_map/all_to_all | solution.py:193
  69.8 0.1 convert_reduce_fusion
  69.9 0.1 collective-permute-start.3
  70.0 1.2 %collective-permute-done.3 = f32[16,128]{1,0:T(8,128)S(1)} collective-permute-done((f32[16,128]{1,0:T(8,128)S(1)}, f32[16,128]{1,0:T(8,128)S(1)}, u32[]{:S(2)}, u32[]{:S(2)}) %collective-permute-start.3) | collective-permute-done | bytes 8224 | tf_op jit(solution)/shard_map/ppermute | solution.py:156
  71.2 1.5 %collective-permute-start.4 = (f32[16,128]{1,0:T(8,128)S(1)}, f32[16,128]{1,0:T(8,128)S(1)}, u32[]{:S(2)}, u32[]{:S(2)}) collective-permute-start(f32[16,128]{1,0:T(8,128)S(1)} %slice_add_fusion), channel_id=1, source_target_pairs={{0,64},{32,96},{64,128},{96,160},{128,192},{160,224},{192,0},{224,... | collective-permute-start | bytes 24584 | tf_op jit(solution)/shard_map/ppermute | solution.py:158
  72.7 2.6 %collective-permute-start.6 = (f32[16,128]{1,0:T(8,128)S(1)}, f32[16,128]{1,0:T(8,128)S(1)}, u32[]{:S(2)}, u32[]{:S(2)}) collective-permute-start(f32[16,128]{1,0:T(8,128)S(1)} %slice_add_fusion), channel_id=1, source_target_pairs={{64,0},{96,32},{128,64},{160,96},{192,128},{224,160},{0,192},{32,2... | collective-permute-start | bytes 24584 | tf_op jit(solution)/shard_map/ppermute | solution.py:160
  75.3 1.6 %collective-permute-done.4 = f32[16,128]{1,0:T(8,128)S(1)} collective-permute-done((f32[16,128]{1,0:T(8,128)S(1)}, f32[16,128]{1,0:T(8,128)S(1)}, u32[]{:S(2)}, u32[]{:S(2)}) %collective-permute-start.4) | collective-permute-done | bytes 8224 | tf_op jit(solution)/shard_map/ppermute | solution.py:158
  77.0 0.3 collective-permute-start.5
  77.3 0.0 collective-permute-done.6
  77.3 5.5 %collective-permute-done.5 = f32[16,128]{1,0:T(8,128)S(1)} collective-permute-done((f32[16,128]{1,0:T(8,128)S(1)}, f32[16,128]{1,0:T(8,128)S(1)}, u32[]{:S(2)}, u32[]{:S(2)}) %collective-permute-start.5) | collective-permute-done | bytes 8224 | tf_op jit(solution)/shard_map/ppermute | solution.py:159
  82.7 0.7 broadcast_in_dim.8
  83.4 5.0 %all-to-all-start.2 = ((f32[32,16,128]{2,1,0:T(8,128)}), f32[32,16,128]{2,1,0:T(8,128)S(1)}, u32[]{:S(2)}, u32[]{:S(2)}) async-start(f32[32,16,128]{2,1,0:T(8,128)} %broadcast_in_dim.8), calls=%async_computation.2 | async-start | bytes 524288 | tf_op jit(solution)/shard_map/all_to_all | solution.py:196
  88.4 0.6 slice.18
  89.0 7.7 %all-to-all-done.2 = f32[32,16,128]{2,1,0:T(8,128)S(1)} async-done(((f32[32,16,128]{2,1,0:T(8,128)}), f32[32,16,128]{2,1,0:T(8,128)S(1)}, u32[]{:S(2)}, u32[]{:S(2)}) %all-to-all-start.2) | async-done | bytes 262176 | tf_op jit(solution)/shard_map/all_to_all | solution.py:196
  96.8 0.7 fusion.1
  (6 shorter events, 0.0 us)
Async XLA Ops:
  0.6 5.5 %copy-start = (bf16[4096,256]{1,0:T(8,128)(2,1)S(1)}, bf16[4096,256]{1,0:T(8,128)(2,1)}, u32[]{:S(2)}) copy-start(bf16[4096,256]{1,0:T(8,128)(2,1)} %param.11) | copy-start | bytes 6291460
  0.6 1.5 %collective-permute-start = (f32[2,128]{1,0:T(2,128)}, f32[2,128]{1,0:T(2,128)S(1)}, u32[]{:S(2)}, u32[]{:S(2)}) collective-permute-start(f32[2,128]{1,0:T(2,128)} %param.14), channel_id=1, source_target_pairs={{0,32},{32,0},{64,96},{96,64},{128,160},{160,128},{192,224},{224,1... | collective-permute-start | bytes 3080 | tf_op jit(solution)/shard_map/ppermute | solution.py:147
  2.9 4.9 %collective-permute-start.1 = (f32[2,256]{1,0:T(2,128)S(1)}, f32[2,256]{1,0:T(2,128)S(1)}, u32[]{:S(2)}, u32[]{:S(2)}) collective-permute-start(f32[2,256]{1,0:T(2,128)S(1)} %maximum_select_fusion.2), channel_id=1, source_target_pairs={{0,64},{32,96},{64,0},{96,32},{128,192},{160,224},{192,128},{224,1... | collective-permute-start | bytes 6152 | tf_op jit(solution)/shard_map/ppermute | solution.py:147
  7.7 16.1 %copy-start.5 = (f32[2,256]{1,0:T(2,128)S(1)}, f32[2,256]{1,0:T(2,128)}, u32[]{:S(2)}) copy-start(f32[2,256]{1,0:T(2,128)} %param.15) | copy-start | bytes 6148
  7.7 16.1 %copy-start.6 = (f32[256]{0:T(256)S(1)}, f32[256]{0:T(256)}, u32[]{:S(2)}) copy-start(f32[256]{0:T(256)} %param.16) | copy-start | bytes 3076
  7.7 27.0 %copy-start.1 = (bf16[256,128]{1,0:T(8,128)(2,1)S(1)}, bf16[256,128]{1,0:T(8,128)(2,1)}, u32[]{:S(2)}) copy-start(bf16[256,128]{1,0:T(8,128)(2,1)} %branch_out_ref.1) | copy-start | bytes 196612
  7.7 27.0 %copy-start.2 = (bf16[256,128]{1,0:T(8,128)(2,1)S(1)}, bf16[256,128]{1,0:T(8,128)(2,1)}, u32[]{:S(2)}) copy-start(bf16[256,128]{1,0:T(8,128)(2,1)} %branch_tan_ref.1) | copy-start | bytes 196612
  7.7 26.9 %copy-start.3 = (bf16[256,128]{1,0:T(8,128)(2,1)S(1)}, bf16[256,128]{1,0:T(8,128)(2,1)}, u32[]{:S(2)}) copy-start(bf16[256,128]{1,0:T(8,128)(2,1)} %trunk_out_ref.1) | copy-start | bytes 196612
  7.7 26.9 %copy-start.4 = (bf16[256,128]{1,0:T(8,128)(2,1)S(1)}, bf16[256,128]{1,0:T(8,128)(2,1)}, u32[]{:S(2)}) copy-start(bf16[256,128]{1,0:T(8,128)(2,1)} %trunk_tan_ref.1) | copy-start | bytes 196612
  8.8 25.8 %all-to-all-start = ((bf16[32,64,256]{2,1,0:T(8,128)(2,1)}), bf16[32,64,256]{2,1,0:T(8,128)(2,1)S(1)}, u32[]{:S(2)}, u32[]{:S(2)}) async-start(bf16[32,64,256]{2,1,0:T(8,128)(2,1)} %broadcast_in_dim.6), calls=%async_computation | async-start | bytes 2097152 | tf_op jit(solution)/shard_map/all_to_all | solution.py:175
  17.7 16.7 %collective-permute-start.2 = (f32[2,512]{1,0:T(2,128)S(1)}, f32[2,512]{1,0:T(2,128)S(1)}, u32[]{:S(2)}, u32[]{:S(2)}) collective-permute-start(f32[2,512]{1,0:T(2,128)S(1)} %maximum_select_fusion.1), channel_id=1, source_target_pairs={{0,128},{32,160},{64,192},{96,224},{128,0},{160,32},{192,64},{224,... | collective-permute-start | bytes 12296 | tf_op jit(solution)/shard_map/ppermute | solution.py:147
  69.9 1.3 %collective-permute-start.3 = (f32[16,128]{1,0:T(8,128)S(1)}, f32[16,128]{1,0:T(8,128)S(1)}, u32[]{:S(2)}, u32[]{:S(2)}) collective-permute-start(f32[16,128]{1,0:T(8,128)S(1)} %slice.19), channel_id=1, source_target_pairs={{0,32},{32,0},{64,96},{96,64},{128,160},{160,128},{192,224},{224,1... | collective-permute-start | bytes 24584 | tf_op jit(solution)/shard_map/ppermute | solution.py:156
  71.2 5.8 %collective-permute-start.4 = (f32[16,128]{1,0:T(8,128)S(1)}, f32[16,128]{1,0:T(8,128)S(1)}, u32[]{:S(2)}, u32[]{:S(2)}) collective-permute-start(f32[16,128]{1,0:T(8,128)S(1)} %slice_add_fusion), channel_id=1, source_target_pairs={{0,64},{32,96},{64,128},{96,160},{128,192},{160,224},{192,0},{224,... | collective-permute-start | bytes 24584 | tf_op jit(solution)/shard_map/ppermute | solution.py:158
  72.7 4.6 %collective-permute-start.6 = (f32[16,128]{1,0:T(8,128)S(1)}, f32[16,128]{1,0:T(8,128)S(1)}, u32[]{:S(2)}, u32[]{:S(2)}) collective-permute-start(f32[16,128]{1,0:T(8,128)S(1)} %slice_add_fusion), channel_id=1, source_target_pairs={{64,0},{96,32},{128,64},{160,96},{192,128},{224,160},{0,192},{32,2... | collective-permute-start | bytes 24584 | tf_op jit(solution)/shard_map/ppermute | solution.py:160
  77.0 5.8 %collective-permute-start.5 = (f32[16,128]{1,0:T(8,128)S(1)}, f32[16,128]{1,0:T(8,128)S(1)}, u32[]{:S(2)}, u32[]{:S(2)}) collective-permute-start(f32[16,128]{1,0:T(8,128)S(1)} %collective-permute-done.4), channel_id=1, source_target_pairs={{0,64},{32,96},{64,128},{96,160},{128,192},{160,224},{192,0},{224,... | collective-permute-start | bytes 24584 | tf_op jit(solution)/shard_map/ppermute | solution.py:159
  83.4 13.3 %all-to-all-start.2 = ((f32[32,16,128]{2,1,0:T(8,128)}), f32[32,16,128]{2,1,0:T(8,128)S(1)}, u32[]{:S(2)}, u32[]{:S(2)}) async-start(f32[32,16,128]{2,1,0:T(8,128)} %broadcast_in_dim.8), calls=%async_computation.2 | async-start | bytes 524288 | tf_op jit(solution)/shard_map/all_to_all | solution.py:196
